TPU v7x, 256 devices: a whole 4x4x8 slice. The times are simulated.
256 devices in a mesh: row: 32 (over y, z), col: 8 (over x, core).
Axes of the slice: x: 4, y: 4, z: 8, core: 2. Of those that a mesh axis runs over, the one named last changes fastest.
Arguments:
- tokens: bfloat16 [1536, 8192], P('row', 'col'), may hold values from -6 to 6
- weight: bfloat16 [8192, 32768], P('col', 'row'), may hold values from -0.109375 to 0.109375
- tile_rows: int32 [32, 8, 32], P('row', 'col'), may hold values from 0 to 63, as said below
- tile_cols: int32 [32, 8, 32], P('row', 'col'), may hold values from 0 to 255, as said below
- tile_count: int32 [32, 8], P('row', 'col'), may hold values from 8 to 32, as said below
- hidden_cotangent: bfloat16 [1536, 32768], P('col', 'row'), may hold values from -6 to 6
Outputs:
- hidden: bfloat16 [1536, 32768], P('col', 'row')
- input_grad: bfloat16 [1536, 8192], P('row', 'col')
- weight_grad: bfloat16 [8192, 32768], P('col', 'row')
Inputs may be any that keep to these rules, and one draw needn't show every extreme that they name: tile_rows[r, c, k] is a row block of the weight (tiles of 128 x 128) among the 8 blocks from c * 8 on, which index c of col holds. tile_cols[r, c, k] is a column block among the 8 blocks from r * 8 on, which index r of row holds; the 32 candidate tiles of one device are distinct. The first tile_count[r, c] candidates of device (r, c) are its nonzero tiles; some device holds 32.
All inputs are finite; a program needn't handle non-finite values.
Results may differ from a plain program's by a relative error of at most 0.0049.
Values may be sent and summed in bfloat16 or wider, within the bound.
No kernel may reach another device: no remote copies, remote signals or barrier semaphores. Data moves between devices by JAX's collectives and lax.ppermute only.
A program may use at most 128 MiB of HBM per device.

v0:
```python
import jax
import jax.numpy as jnp
from jax import lax
from jax.sharding import Mesh
from jax.sharding import PartitionSpec as P

TILE = 128
ROW = ("row_0", "row_1")


def laid_out(pieces, dim):
    pieces = jnp.moveaxis(pieces, 0, dim)
    dims = pieces.shape
    return pieces.reshape(*dims[:dim], dims[dim] * dims[dim + 1], *dims[dim + 2 :])


def all_blocks(shard, axes, turns):
    pieces = shard
    for k in turns:
        pieces = lax.all_gather(pieces, axes[k])
    done = turns[::-1]
    back = [done.index(k) for k in range(len(axes))]
    pieces = pieces.transpose(*back, *range(len(axes), pieces.ndim))
    return pieces.reshape(-1, *shard.shape)


def gathered_by_axis(shard, axes, turns, dim):
    return laid_out(all_blocks(shard, axes, turns), dim)


def own_rows(so_far, axes):
    for axis in axes:
        so_far = lax.psum_scatter(so_far, axis, scatter_dimension=0, tiled=True)
    return so_far


def sparse_apply(inputs, live_tiles, in_index, out_index, out_blocks, flipped):
    count_rows, in_width = inputs.shape
    in_blocks = in_width // TILE
    block_rows = 128
    picker = (in_index[:, None] == jnp.arange(in_blocks)[None, :]).astype(jnp.bfloat16)
    placer = (out_index[:, None] == jnp.arange(out_blocks)[None, :]).astype(jnp.float32)

    def per_block(rows_block):
        shaped_rows = rows_block.reshape(block_rows, in_blocks, TILE)
        pieces = jnp.einsum(
            "bjp,kj->bkp", shaped_rows, picker, preferred_element_type=jnp.float32
        ).astype(jnp.bfloat16)
        if flipped:
            product = jnp.einsum(
                "bkq,kpq->bkp", pieces, live_tiles, preferred_element_type=jnp.float32
            )
        else:
            product = jnp.einsum(
                "bkp,kpq->bkq", pieces, live_tiles, preferred_element_type=jnp.float32
            )
        placed = jnp.einsum("bkq,kc->bcq", product, placer, precision=lax.Precision.HIGHEST)
        return placed.reshape(block_rows, out_blocks * TILE)

    stacked = inputs.reshape(count_rows // block_rows, block_rows, in_width)
    return lax.map(per_block, stacked).reshape(count_rows, out_blocks * TILE)


def tile_grads(full_tokens, full_grads, local_rows, local_cols, is_live, row_blocks, col_blocks):
    count_rows = full_tokens.shape[0]
    block_rows = 128
    steps_count = count_rows // block_rows
    left_side = full_tokens.reshape(steps_count, block_rows, row_blocks, TILE)
    right_side = full_grads.reshape(steps_count, block_rows, col_blocks, TILE)

    def accumulate(running, block_pair):
        token_block, grad_block = block_pair
        product = jnp.einsum(
            "bkp,bkq->kpq",
            token_block[:, local_rows],
            grad_block[:, local_cols],
            preferred_element_type=jnp.float32,
        )
        return (running + product, None)

    start_sums = jnp.zeros((local_rows.shape[0], TILE, TILE), jnp.float32)
    tile_sums, leftover = lax.scan(accumulate, start_sums, (left_side, right_side))
    tile_sums = tile_sums * is_live[:, None, None].astype(jnp.float32)
    slot_ids = local_rows * col_blocks + local_cols
    placed = (
        jnp.zeros((row_blocks * col_blocks, TILE, TILE), jnp.float32).at[slot_ids].add(tile_sums)
    )
    placed = placed.reshape(row_blocks, col_blocks, TILE, TILE).transpose(0, 2, 1, 3)
    return placed.reshape(row_blocks * TILE, col_blocks * TILE).astype(jnp.bfloat16)


def on_device(tokens, weight, tile_rows, tile_cols, tile_count, hidden_cotangent):
    row_index = lax.axis_index(ROW)
    col_index = lax.axis_index("col")
    row_blocks = weight.shape[0] // TILE
    col_blocks = weight.shape[1] // TILE
    capacity = tile_rows.shape[2]
    local_rows = tile_rows.reshape(capacity) - col_index * row_blocks
    local_cols = tile_cols.reshape(capacity) - row_index * col_blocks
    is_live = jnp.arange(capacity) < tile_count.reshape(())
    shaped = weight.reshape(row_blocks, TILE, col_blocks, TILE)
    live_tiles = shaped[local_rows, :, local_cols, :] * is_live[:, None, None].astype(jnp.bfloat16)
    full_tokens = gathered_by_axis(tokens, ROW, (0, 1), 0)
    pre_act = lax.psum_scatter(
        sparse_apply(full_tokens, live_tiles, local_rows, local_cols, col_blocks, False),
        "col",
        scatter_dimension=0,
        tiled=True,
    )
    gate_value = jax.nn.sigmoid(pre_act)
    hidden = (pre_act * gate_value).astype(jnp.bfloat16)
    silu_slope = gate_value * (1.0 + pre_act * (1.0 - gate_value))
    grad_pre = (hidden_cotangent.astype(jnp.float32) * silu_slope).astype(jnp.bfloat16)
    full_grads = lax.all_gather(grad_pre, "col", axis=0, tiled=True)
    input_grad = own_rows(
        sparse_apply(full_grads, live_tiles, local_cols, local_rows, row_blocks, True), ROW
    ).astype(jnp.bfloat16)
    weight_grad = tile_grads(
        full_tokens, full_grads, local_rows, local_cols, is_live, row_blocks, col_blocks
    )
    return (hidden, input_grad, weight_grad)


def solution(mesh):
    split = Mesh(mesh.devices.reshape(4, 8, mesh.shape["col"]), ("row_0", "row_1", "col"))
    placed = (
        P(ROW, "col"),
        P("col", ROW),
        P(ROW, "col", None),
        P(ROW, "col", None),
        P(ROW, "col"),
        P("col", ROW),
    )
    return jax.shard_map(
        on_device,
        mesh=split,
        in_specs=placed,
        out_specs=(P("col", ROW), P(ROW, "col"), P("col", ROW)),
        check_vma=False,
    )
```

profile of v0, /device:TPU:1, one launch (start us, length us, event | category | flops | bytes accessed | tf_op | source)
XLA Modules:
  0.0 455.6 jit_solution(8898258210480005376)
XLA Ops:
  7.2 13.0 %all-gather = bf16[192,1024]{1,0:T(8,128)(2,1)} all-gather(bf16[48,1024]{1,0:T(8,128)(2,1)} %param.12), channel_id=2, replica_groups=mesh['row_0'=4,'row_1'=8,'col'=8] {'row_0'}, dimensions={0}, use_global_device_ids=true | all-gather | bytes 491520 | tf_op jit(solution)/shard_map/all_gather | solution.py:20
  24.8 44.5 %all-gather.7.cloned.1.call-done = bf16[32,48,1024]{2,1,0:T(8,128)(2,1)} async-done(((bf16[4,48,1024]{2,1,0:T(8,128)(2,1)}), bf16[32,48,1024]{2,1,0:T(8,128)(2,1)}) %all-gather.7.cloned.1.call-update) | async-done | bytes 3145744 | tf_op jit(solution)/shard_map/all_gather | solution.py:20
  69.2 4.1 copy.27
  73.3 3.5 broadcast.138.clone
  76.8 66.5 %while.33 = (s32[]{:T(128)}, f32[12,128,1024]{2,1,0:T(8,128)}, bf16[12,128,1024]{2,1,0:T(8,128)(2,1)}, bf16[32,128,128]{2,1,0:T(8,128)(2,1)S(1)}, s32[32]{0:T(128)S(1)}, /*index=5*/s32[32]{0:T(128)S(1)}, s32[]{:T(128)}) while((s32[]{:T(128)}, f32[12,128,1024]{2,1,0:T(8,128)}, bf16[12,128,1024]{2,1,0:T(8,128)(2,1)}, ...), condition=%wide.region_1.2_spmd.clone, body=%wide.region_0.1_spmd.clone.sunk | while | flops 193463296 | bytes 11273041 | solution.py:61
  79.0 2.4 fusion.79
  84.5 2.4 fusion.79
  90.1 2.4 fusion.79
  95.6 2.4 fusion.79
  101.2 2.4 fusion.79
  106.7 2.4 fusion.79
  112.3 2.4 fusion.79
  117.8 2.4 fusion.79
  123.3 2.4 fusion.79
  128.9 2.4 fusion.79
  134.4 2.4 fusion.79
  140.0 2.4 fusion.79
  143.4 43.4 %reduce-scatter.4.cloned.1.call-done = f32[192,1024]{1,0:T(8,128)} async-done(((f32[1536,1024]{1,0:T(8,128)}), f32[192,1024]{1,0:T(8,128)}) %reduce-scatter.4.cloned.1.call-update) | async-done | bytes 786448 | tf_op jit(solution)/shard_map/reduce_scatter | solution.py:104
  186.8 2.4 multiply_convert_fusion
  189.2 31.1 %all-gather.5.cloned.1.call-done = bf16[1536,1024]{1,0:T(8,128)(2,1)} async-done(((bf16[192,1024]{1,0:T(8,128)(2,1)}), bf16[1536,1024]{1,0:T(8,128)(2,1)}) %all-gather.5.cloned.1.call-update) | async-done | bytes 3145744 | tf_op jit(solution)/shard_map/all_gather | solution.py:114
  220.3 3.5 broadcast.138
  223.8 68.4 %while.34 = (s32[]{:T(128)}, f32[12,128,1024]{2,1,0:T(8,128)}, bf16[12,128,1024]{2,1,0:T(8,128)(2,1)}, bf16[32,128,128]{2,1,0:T(8,128)(2,1)S(1)}, s32[32]{0:T(128)S(1)}, /*index=5*/s32[32]{0:T(128)S(1)}, s32[]{:T(128)}) while((s32[]{:T(128)}, f32[12,128,1024]{2,1,0:T(8,128)}, bf16[12,128,1024]{2,1,0:T(8,128)(2,1)}, ...), condition=%wide.region_4.5_spmd.clone, body=%wide.region_3.4_spmd.clone.sunk | while | flops 193463296 | bytes 11273041 | solution.py:61
  226.2 2.4 fusion.87
  237.6 2.4 fusion.87
  249.0 2.4 fusion.87
  254.7 2.4 fusion.87
  266.1 2.4 fusion.87
  271.8 2.4 fusion.87
  283.2 2.4 fusion.87
  288.9 2.4 fusion.87
  294.1 2.6 copy.39
  296.7 2.5 copy.40
  299.1 59.5 %reduce-scatter.6.cloned.1.call-done = f32[384,1024]{1,0:T(8,128)} async-done(((f32[1536,1024]{1,0:T(8,128)}), f32[384,1024]{1,0:T(8,128)}) %reduce-scatter.6.cloned.1.call-update) | async-done | bytes 1572880 | tf_op jit(solution)/shard_map/reduce_scatter | solution.py:33
  358.6 72.4 %while.35 = (s32[]{:T(128)}, f32[32,128,128]{2,1,0:T(8,128)}, bf16[12,128,8,128]{3,2,1,0:T(8,128)(2,1)}, s32[32]{0:T(128)S(1)}, bf16[12,128,8,128]{3,2,1,0:T(8,1...) while((s32[]{:T(128)}, f32[32,128,128]{2,1,0:T(8,128)}, bf16[12,128,8,128]{3,2,1,0:T(8,128)(2,1)}, ...), condition=%wide.region_8.9_spmd.clone, body=%wide.region_7.8_spmd.clone.sunk | while | flops 135268544 | bytes 12592227 | solution.py:82
  365.9 3.4 select_add_fusion.2
  372.1 3.5 select_add_fusion.2
  378.3 3.5 select_add_fusion.2
  384.5 3.5 select_add_fusion.2
  390.6 3.5 select_add_fusion.2
  396.8 3.4 select_add_fusion.2
  403.0 3.4 select_add_fusion.2
  409.1 3.4 select_add_fusion.2
  415.3 3.4 select_add_fusion.2
  421.4 3.4 select_add_fusion.2
  427.6 3.4 select_add_fusion.2
  432.8 2.5 broadcast_in_dim.11
  435.3 6.3 %scatter_fusion = f32[64,128,128]{2,1,0:T(8,128)} fusion(f32[64,128,128]{2,1,0:T(8,128)} %broadcast_in_dim.11, s32[32]{0:T(128)S(1)} %get-tuple-element.217, f32[32,128,128]{2,1,0:T(8,128)S(1)} %broadcast_multiply_fusion), kind=kCustom, calls=%fused_computation.3 | custom fusion | flops 524288 | bytes 6291584 | tf_op jit(solution)/shard_map/scatter-add | solution.py:86
  441.6 2.6 convert_element_type.74
  (279 shorter events, 133.0 us)
Async XLA Ops:
  7.2 62.1 %all-gather.7.cloned.1.call-start = ((), (), s32[]{:S(2)}) async-start(), calls=%async_computation.7 | async-start | bytes 3538944 | tf_op jit(solution)/shard_map/all_gather | solution.py:20
  20.2 166.5 %reduce-scatter.4.cloned.1.call-start = ((), (), s32[]{:S(2)}) async-start(), calls=%async_computation.3 | async-start | bytes 7077888 | tf_op jit(solution)/shard_map/reduce_scatter | solution.py:104
  22.5 1.3 copy-start.3
  22.5 1.3 copy-start.4
  143.3 43.5 %copy-start.2 = (bf16[192,1024]{1,0:T(8,128)(2,1)S(1)}, bf16[192,1024]{1,0:T(8,128)(2,1)}, u32[]{:S(2)}) copy-start(bf16[192,1024]{1,0:T(8,128)(2,1)} %param.17) | copy-start | bytes 1179652
  143.3 77.0 %all-gather.5.cloned.1.call-start = ((), (), s32[]{:S(2)}) async-start(), calls=%async_computation.4 | async-start | bytes 3538944 | tf_op jit(solution)/shard_map/all_gather | solution.py:114
  189.2 169.4 %reduce-scatter.6.cloned.1.call-start = ((), (), s32[]{:S(2)}) async-start(), calls=%async_computation.5 | async-start | bytes 7864320 | tf_op jit(solution)/shard_map/reduce_scatter | solution.py:33
  292.2 1.9 copy-start
  292.2 155.3 %reduce-scatter.8.cloned.1.call-start = ((), (), s32[]{:S(2)}) async-start(), calls=%async_computation.6 | async-start | bytes 1769472 | tf_op jit(solution)/shard_map/reduce_scatter | solution.py:33
  294.1 2.6 copy-start.1
Sparse Core Ops, SparseCore 0:
  20.4 48.8 all-gather.6
  143.4 43.3 reduce-scatter.3
  189.3 30.9 all-gather.4
  292.4 66.2 reduce-scatter.5
  361.0 35.9 reduce-scatter.7
where the time goes:
time: 457 us; the launch traced here: 456 us
  waiting for transfers between devices  179 us (39%)
  matrix products  127 us (28%)
  local copies, waits for them, and re-layouts  105 us (23%)
  other arithmetic  14.9 us (3%)
  between operations  14.6 us (3%)
  blocking collectives  13 us (3%)
    reduce_scatter x2, waiting for transfers between devices, own_rows(): so_far = lax.psum_scatter(so_far, axis, scatter_dimension=0, tiled=True)  59.5 us
    dot_general x24, matrix products, per_block(): jnp.einsum('bkq,kc->bcq', product, placer, precision=lax.Precision.HIGHEST)  56.6 us
    all_gather x1, waiting for transfers between devices, all_blocks(): pieces = lax.all_gather(pieces, axes[k])  44.5 us
    reduce_scatter x1, waiting for transfers between devices, on_device(): lax.psum_scatter(sparse_apply(full_tokens, live_tiles, local_rows, local_...  43.4 us
    dot_general x12, matrix products, accumulate(): jnp.einsum('bkp,bkq->kpq', token_block[:, local_rows], grad_block[:, loca...  39.8 us
    all_gather x1, waiting for transfers between devices, on_device(): full_grads = lax.all_gather(grad_pre, 'col', axis=0, tiled=True)  31.1 us
    while x48, local copies, waits for them, and re-layouts  24.3 us
    dynamic_update_slice x24, local copies, waits for them, and re-layouts, sparse_apply(): return lax.map(per_block, stacked).reshape(count_rows, out_blocks * TILE)  20.5 us
  transfers between devices with their start and end apart: 5, of which 4 were waited for; matrix products, arithmetic and copies ran while one was open for 21% of the time, Pallas kernels for 0%

commit v1 on v0

--- a/solution.py
+++ b/solution.py
@@ -6,6 +6,21 @@
 
 TILE = 128
 ROW = ("row_0", "row_1")
+
+
+def flows_detail(a0):
+    n_dev_all = lax.axis_size("col")
+    lanes = tuple(((p, (p + 1) % n_dev_all) for p in range(n_dev_all)))
+
+    def play_state(all_rows):
+        if len(all_rows) == n_dev_all:
+            return all_rows
+        wide_out = play_state([lax.ppermute(all_rows[0], perm=lanes, axis_name="col"), *all_rows])
+        return wide_out
+
+    moved = jnp.concatenate(play_state([a0]), axis=0)
+    x_now = jnp.roll(moved, (lax.axis_index("col") + 1) * a0.shape[0], axis=0)
+    return x_now
 
 
 def laid_out(pieces, dim):
@@ -111,7 +126,7 @@
     hidden = (pre_act * gate_value).astype(jnp.bfloat16)
     silu_slope = gate_value * (1.0 + pre_act * (1.0 - gate_value))
     grad_pre = (hidden_cotangent.astype(jnp.float32) * silu_slope).astype(jnp.bfloat16)
-    full_grads = lax.all_gather(grad_pre, "col", axis=0, tiled=True)
+    full_grads = flows_detail(grad_pre)
     input_grad = own_rows(
         sparse_apply(full_grads, live_tiles, local_cols, local_rows, row_blocks, True), ROW
     ).astype(jnp.bfloat16)

time: 457 us -> 493 us (1.079)
  waiting for transfers between devices: 179 us -> 196 us
  starting transfers between devices: 0.39 us -> 9.85 us
  local copies, waits for them, and re-layouts: 105 us -> 113 us
    ppermute x0 -> x7, waiting for transfers between devices: none -> 44.1 us  [play_state(): lax.ppermute(all_rows[0], perm=lanes, axis_name='col')]
    all_gather x1 -> x0, waiting for transfers between devices: 31.1 us -> none  [on_device(): full_grads = lax.all_gather(grad_pre, 'col', axis=0, tiled=True)]
    ppermute x0 -> x7, starting transfers between devices: none -> 9.28 us  [play_state(): lax.ppermute(all_rows[0], perm=lanes, axis_name='col')]
    unnamed x14 -> x32, local copies, waits for them, and re-layouts: 10.8 us -> 16.1 us
  transfers between devices with their start and end apart: 5 -> 11, of which waited for: 4 -> 10; matrix products, arithmetic and copies ran while one was open for 21% -> 20% of each run, Pallas kernels for 0% -> 0%
where the time goes in v1:
time: 493 us; the launch traced here: 491 us
  waiting for transfers between devices  196 us (40%)
  matrix products  127 us (26%)
  local copies, waits for them, and re-layouts  113 us (23%)
  other arithmetic  14.8 us (3%)
  between operations  14.7 us (3%)
  blocking collectives  13 us (3%)
  starting transfers between devices  9.85 us (2%)
    reduce_scatter x2, waiting for transfers between devices, own_rows(): so_far = lax.psum_scatter(so_far, axis, scatter_dimension=0, tiled=True)  64.2 us
    dot_general x24, matrix products, per_block(): jnp.einsum('bkq,kc->bcq', product, placer, precision=lax.Precision.HIGHEST)  56.6 us
    all_gather x1, waiting for transfers between devices, all_blocks(): pieces = lax.all_gather(pieces, axes[k])  44.5 us
    ppermute x7, waiting for transfers between devices, play_state(): lax.ppermute(all_rows[0], perm=lanes, axis_name='col')  44.1 us
    reduce_scatter x1, waiting for transfers between devices, on_device(): lax.psum_scatter(sparse_apply(full_tokens, live_tiles, local_rows, local_...  43.2 us
    dot_general x12, matrix products, accumulate(): jnp.einsum('bkp,bkq->kpq', token_block[:, local_rows], grad_block[:, loca...  39.8 us
    while x48, local copies, waits for them, and re-layouts  24.3 us
    dynamic_update_slice x24, local copies, waits for them, and re-layouts, sparse_apply(): return lax.map(per_block, stacked).reshape(count_rows, out_blocks * TILE)  20.3 us
  transfers between devices with their start and end apart: 11, of which 10 were waited for; matrix products, arithmetic and copies ran while one was open for 20% of the time, Pallas kernels for 0%

profile of v1, /device:TPU:1, one launch (start us, length us, event | category | flops | bytes accessed | tf_op | source)
XLA Modules:
  0.0 490.6 jit_solution(17066835462938625140)
XLA Ops:
  7.2 13.0 %all-gather = bf16[192,1024]{1,0:T(8,128)(2,1)} all-gather(bf16[48,1024]{1,0:T(8,128)(2,1)} %param.12), channel_id=2, replica_groups=mesh['row_0'=4,'row_1'=8,'col'=8] {'row_0'}, dimensions={0}, use_global_device_ids=true | all-gather | bytes 491520 | tf_op jit(solution)/shard_map/all_gather | solution.py:35
  24.8 44.5 %all-gather.4.cloned.1.call-done = bf16[32,48,1024]{2,1,0:T(8,128)(2,1)} async-done(((bf16[4,48,1024]{2,1,0:T(8,128)(2,1)}), bf16[32,48,1024]{2,1,0:T(8,128)(2,1)}) %all-gather.4.cloned.1.call-update) | async-done | bytes 3145744 | tf_op jit(solution)/shard_map/all_gather | solution.py:35
  69.3 4.0 copy.26
  73.3 3.5 broadcast.138.clone
  76.7 66.3 %while.33 = (s32[]{:T(128)}, f32[12,128,1024]{2,1,0:T(8,128)}, bf16[12,128,1024]{2,1,0:T(8,128)(2,1)}, bf16[32,128,128]{2,1,0:T(8,128)(2,1)S(1)}, s32[32]{0:T(128)S(1)}, /*index=5*/s32[32]{0:T(128)S(1)}, s32[]{:T(128)}) while((s32[]{:T(128)}, f32[12,128,1024]{2,1,0:T(8,128)}, bf16[12,128,1024]{2,1,0:T(8,128)(2,1)}, ...), condition=%wide.region_1.2_spmd.clone, body=%wide.region_0.1_spmd.clone.sunk | while | flops 193463296 | bytes 11273041 | solution.py:76
  79.0 2.4 fusion.80
  84.5 2.4 fusion.80
  90.0 2.4 fusion.80
  101.1 2.4 fusion.80
  106.6 2.4 fusion.80
  112.1 2.4 fusion.80
  117.6 2.4 fusion.80
  123.2 2.4 fusion.80
  128.7 2.4 fusion.80
  134.2 2.4 fusion.80
  139.8 2.4 fusion.80
  143.3 43.2 %reduce-scatter.4.cloned.1.call-done = f32[192,1024]{1,0:T(8,128)} async-done(((f32[1536,1024]{1,0:T(8,128)}), f32[192,1024]{1,0:T(8,128)}) %reduce-scatter.4.cloned.1.call-update) | async-done | bytes 786448 | tf_op jit(solution)/shard_map/reduce_scatter | solution.py:119
  189.1 4.7 collective-permute-done
  193.8 2.5 collective-permute-start.1
  196.3 4.7 collective-permute-done.1
  201.0 2.5 collective-permute-start.2
  203.5 4.7 collective-permute-done.2
  208.2 2.5 collective-permute-start.3
  210.7 5.8 %collective-permute-done.3 = bf16[192,1024]{1,0:T(8,128)(2,1)S(1)} collective-permute-done((bf16[192,1024]{1,0:T(8,128)(2,1)S(1)}, bf16[192,1024]{1,0:T(8,128)(2,1)S(1)}, u32[]{:S(2)}, u32[]{:S(2)}) %collective-permute-start.3) | collective-permute-done | bytes 393248 | tf_op jit(solution)/shard_map/ppermute | solution.py:18
  217.9 7.0 %collective-permute-done.4 = bf16[192,1024]{1,0:T(8,128)(2,1)S(1)} collective-permute-done((bf16[192,1024]{1,0:T(8,128)(2,1)S(1)}, bf16[192,1024]{1,0:T(8,128)(2,1)S(1)}, u32[]{:S(2)}, u32[]{:S(2)}) %collective-permute-start.4) | collective-permute-done | bytes 393248 | tf_op jit(solution)/shard_map/ppermute | solution.py:18
  225.1 8.4 %collective-permute-done.5 = bf16[192,1024]{1,0:T(8,128)(2,1)} collective-permute-done((bf16[192,1024]{1,0:T(8,128)(2,1)S(1)}, bf16[192,1024]{1,0:T(8,128)(2,1)}, u32[]{:S(2)}, u32[]{:S(2)}) %collective-permute-start.5) | collective-permute-done | bytes 393248 | tf_op jit(solution)/shard_map/ppermute | solution.py:18
  233.4 8.7 %collective-permute-done.6 = bf16[192,1024]{1,0:T(8,128)(2,1)} collective-permute-done((bf16[192,1024]{1,0:T(8,128)(2,1)}, bf16[192,1024]{1,0:T(8,128)(2,1)}, u32[]{:S(2)}, u32[]{:S(2)}) %collective-permute-start.6) | collective-permute-done | bytes 393248 | tf_op jit(solution)/shard_map/ppermute | solution.py:18
  246.7 3.0 constant_dynamic-slice_fusion.2
  249.7 3.4 broadcast.138
  253.1 68.4 %while.34 = (s32[]{:T(128)}, f32[12,128,1024]{2,1,0:T(8,128)}, bf16[12,128,1024]{2,1,0:T(8,128)(2,1)}, bf16[32,128,128]{2,1,0:T(8,128)(2,1)S(1)}, s32[32]{0:T(128)S(1)}, /*index=5*/s32[32]{0:T(128)S(1)}, s32[]{:T(128)}) while((s32[]{:T(128)}, f32[12,128,1024]{2,1,0:T(8,128)}, bf16[12,128,1024]{2,1,0:T(8,128)(2,1)}, ...), condition=%wide.region_4.5_spmd.clone, body=%wide.region_3.4_spmd.clone.sunk | while | flops 193463296 | bytes 11273041 | solution.py:76
  323.4 2.5 copy.38
  327.0 2.5 copy.39
  329.4 64.2 %reduce-scatter.6.cloned.1.call-done = f32[384,1024]{1,0:T(8,128)} async-done(((f32[1536,1024]{1,0:T(8,128)}), f32[384,1024]{1,0:T(8,128)}) %reduce-scatter.6.cloned.1.call-update) | async-done | bytes 1572880 | tf_op jit(solution)/shard_map/reduce_scatter | solution.py:48
  393.7 72.4 %while.35 = (s32[]{:T(128)}, f32[32,128,128]{2,1,0:T(8,128)}, bf16[12,128,8,128]{3,2,1,0:T(8,128)(2,1)}, s32[32]{0:T(128)S(1)}, bf16[12,128,8,128]{3,2,1,0:T(8,1...) while((s32[]{:T(128)}, f32[32,128,128]{2,1,0:T(8,128)}, bf16[12,128,8,128]{3,2,1,0:T(8,128)(2,1)}, ...), condition=%wide.region_8.9_spmd.clone, body=%wide.region_7.8_spmd.clone.sunk | while | flops 135268544 | bytes 12592227 | solution.py:97
  401.0 3.4 select_add_fusion.2
  407.1 3.5 select_add_fusion.2
  413.3 3.5 select_add_fusion.2
  419.5 3.5 select_add_fusion.2
  425.7 3.5 select_add_fusion.2
  431.9 3.4 select_add_fusion.2
  438.0 3.4 select_add_fusion.2
  444.2 3.4 select_add_fusion.2
  450.3 3.4 select_add_fusion.2
  456.5 3.4 select_add_fusion.2
  462.7 3.4 select_add_fusion.2
  467.9 2.5 broadcast_in_dim.11
  470.4 6.2 %scatter_fusion = f32[64,128,128]{2,1,0:T(8,128)} fusion(f32[64,128,128]{2,1,0:T(8,128)} %broadcast_in_dim.11, s32[32]{0:T(128)S(1)} %get-tuple-element.211, f32[32,128,128]{2,1,0:T(8,128)S(1)} %broadcast_multiply_fusion), kind=kCustom, calls=%fused_computation.3 | custom fusion | flops 524288 | bytes 6291584 | tf_op jit(solution)/shard_map/scatter-add | solution.py:101
  476.6 2.6 convert_element_type.74
  (310 shorter events, 163.7 us)
Async XLA Ops:
  7.2 16.6 %copy-start.4 = (s32[1,1,32]{2,1,0:T(1,128)S(1)}, s32[1,1,32]{2,1,0:T(1,128)}, u32[]{:S(2)}) copy-start(s32[1,1,32]{2,1,0:T(1,128)} %param.14) | copy-start | bytes 388
  7.2 16.6 %copy-start.5 = (s32[1,1,32]{2,1,0:T(1,128)S(1)}, s32[1,1,32]{2,1,0:T(1,128)}, u32[]{:S(2)}) copy-start(s32[1,1,32]{2,1,0:T(1,128)} %param.15) | copy-start | bytes 388
  7.2 62.1 %all-gather.4.cloned.1.call-start = ((), (), s32[]{:S(2)}) async-start(), calls=%async_computation.6 | async-start | bytes 3538944 | tf_op jit(solution)/shard_map/all_gather | solution.py:35
  20.3 166.3 %reduce-scatter.4.cloned.1.call-start = ((), (), s32[]{:S(2)}) async-start(), calls=%async_computation.3 | async-start | bytes 7077888 | tf_op jit(solution)/shard_map/reduce_scatter | solution.py:119
  143.1 43.5 %copy-start.3 = (bf16[192,1024]{1,0:T(8,128)(2,1)S(1)}, bf16[192,1024]{1,0:T(8,128)(2,1)}, u32[]{:S(2)}) copy-start(bf16[192,1024]{1,0:T(8,128)(2,1)} %param.17) | copy-start | bytes 1179652
  143.1 250.6 %reduce-scatter.6.cloned.1.call-start = ((), (), s32[]{:S(2)}) async-start(), calls=%async_computation.4 | async-start | bytes 7864320 | tf_op jit(solution)/shard_map/reduce_scatter | solution.py:48
  188.8 5.0 %collective-permute-start = (bf16[192,1024]{1,0:T(8,128)(2,1)S(1)}, bf16[192,1024]{1,0:T(8,128)(2,1)S(1)}, u32[]{:S(2)}, u32[]{:S(2)}) collective-permute-start(bf16[192,1024]{1,0:T(8,128)(2,1)S(1)} %get-tuple-element.209), channel_id=1, source_target_pairs={{0,1},{1,2},{2,3},{3,4},{4,5},{5,6},{6,7},{7,0},{8,9},{9,10},{10,1... | collective-permute-start | bytes 1179656 | tf_op jit(solution)/shard_map/ppermute | solution.py:18
  193.8 7.2 %collective-permute-start.1 = (bf16[192,1024]{1,0:T(8,128)(2,1)S(1)}, bf16[192,1024]{1,0:T(8,128)(2,1)S(1)}, u32[]{:S(2)}, u32[]{:S(2)}) collective-permute-start(bf16[192,1024]{1,0:T(8,128)(2,1)S(1)} %collective-permute-done), channel_id=1, source_target_pairs={{0,1},{1,2},{2,3},{3,4},{4,5},{5,6},{6,7},{7,0},{8,9},{9,10},{10,1... | collective-permute-start | bytes 1179656 | tf_op jit(solution)/shard_map/ppermute | solution.py:18
  201.0 7.2 %collective-permute-start.2 = (bf16[192,1024]{1,0:T(8,128)(2,1)S(1)}, bf16[192,1024]{1,0:T(8,128)(2,1)S(1)}, u32[]{:S(2)}, u32[]{:S(2)}) collective-permute-start(bf16[192,1024]{1,0:T(8,128)(2,1)S(1)} %collective-permute-done.1), channel_id=1, source_target_pairs={{0,1},{1,2},{2,3},{3,4},{4,5},{5,6},{6,7},{7,0},{8,9},{9,10},{10,1... | collective-permute-start | bytes 1179656 | tf_op jit(solution)/shard_map/ppermute | solution.py:18
  208.2 8.3 %collective-permute-start.3 = (bf16[192,1024]{1,0:T(8,128)(2,1)S(1)}, bf16[192,1024]{1,0:T(8,128)(2,1)S(1)}, u32[]{:S(2)}, u32[]{:S(2)}) collective-permute-start(bf16[192,1024]{1,0:T(8,128)(2,1)S(1)} %collective-permute-done.2), channel_id=1, source_target_pairs={{0,1},{1,2},{2,3},{3,4},{4,5},{5,6},{6,7},{7,0},{8,9},{9,10},{10,1... | collective-permute-start | bytes 1179656 | tf_op jit(solution)/shard_map/ppermute | solution.py:18
  216.5 8.4 %collective-permute-start.4 = (bf16[192,1024]{1,0:T(8,128)(2,1)S(1)}, bf16[192,1024]{1,0:T(8,128)(2,1)S(1)}, u32[]{:S(2)}, u32[]{:S(2)}) collective-permute-start(bf16[192,1024]{1,0:T(8,128)(2,1)S(1)} %collective-permute-done.3), channel_id=1, source_target_pairs={{0,1},{1,2},{2,3},{3,4},{4,5},{5,6},{6,7},{7,0},{8,9},{9,10},{10,1... | collective-permute-start | bytes 1179656 | tf_op jit(solution)/shard_map/ppermute | solution.py:18
  224.9 8.5 %collective-permute-start.5 = (bf16[192,1024]{1,0:T(8,128)(2,1)S(1)}, bf16[192,1024]{1,0:T(8,128)(2,1)}, u32[]{:S(2)}, u32[]{:S(2)}) collective-permute-start(bf16[192,1024]{1,0:T(8,128)(2,1)S(1)} %collective-permute-done.4), channel_id=1, source_target_pairs={{0,1},{1,2},{2,3},{3,4},{4,5},{5,6},{6,7},{7,0},{8,9},{9,10},{10,1... | collective-permute-start | bytes 1179656 | tf_op jit(solution)/shard_map/ppermute | solution.py:18
  233.4 8.7 %collective-permute-start.6 = (bf16[192,1024]{1,0:T(8,128)(2,1)}, bf16[192,1024]{1,0:T(8,128)(2,1)}, u32[]{:S(2)}, u32[]{:S(2)}) collective-permute-start(bf16[192,1024]{1,0:T(8,128)(2,1)} %collective-permute-done.5), channel_id=1, source_target_pairs={{0,1},{1,2},{2,3},{3,4},{4,5},{5,6},{6,7},{7,0},{8,9},{9,10},{10,1... | collective-permute-start | bytes 1179656 | tf_op jit(solution)/shard_map/ppermute | solution.py:18
  246.7 6.4 %copy-start.1 = (bf16[3072,1024]{1,0:T(8,128)(2,1)}, bf16[3072,1024]{1,0:T(8,128)(2,1)S(1)}, u32[]{:S(2)}) copy-start(bf16[3072,1024]{1,0:T(8,128)(2,1)S(1)} %constant_dynamic-update-slice_fusion.2) | copy-start | bytes 18874372
  321.5 1.9 copy-start
  321.6 160.9 %reduce-scatter.8.cloned.1.call-start = ((), (), s32[]{:S(2)}) async-start(), calls=%async_computation.5 | async-start | bytes 1769472 | tf_op jit(solution)/shard_map/reduce_scatter | solution.py:48
  321.8 4.1 copy-start.2
Sparse Core Ops, SparseCore 0:
  20.4 48.8 all-gather.3
  143.2 43.3 reduce-scatter.3
  321.7 71.9 reduce-scatter.5
  396.1 36.0 reduce-scatter.7
